TPU v7x, 32 devices: a whole 2x2x4 slice. The times are simulated.
32 devices in a mesh: dp: 8 (over y, x, core), seg: 4 (over z).
Axes of the slice: x: 2, y: 2, z: 4, core: 2. Of those that a mesh axis runs over, the one named last changes fastest.
Arguments:
- tokens: bfloat16 [2, 16, 2048, 768], P(None, 'dp', 'seg'), may hold values from -6 to 6
- cotangent: bfloat16 [2, 16, 2048, 768], P(None, 'dp', 'seg'), may hold values from -6 to 6
- document_ids: int32 [2, 16, 16], P(None, 'dp'), may hold values from 0 to 3, never falling along the last dimension, each value on 1 to 8 neighbouring positions
- position_ids: int32 [2, 16, 16], P(None, 'dp'), may hold values from 0 to 63
- project_in: bfloat16 [2, 768, 2304], P(None, 'dp', 'seg'), may hold values from -0.3125 to 0.3125
- project_out: bfloat16 [2, 768, 768], P(None, 'dp', 'seg'), may hold values from -0.875 to 0.875
- up_weight: bfloat16 [2, 768, 3072], P(None, 'dp', 'seg'), may hold values from -0.21875 to 0.21875
- down_weight: bfloat16 [2, 3072, 768], P(None, 'dp', 'seg'), may hold values from -0.109375 to 0.109375
- norm_gains: bfloat16 [2, 768, 2], P(None, 'dp'), may hold values from 0.5 to 1.5
- biases: bfloat16 [2, 768, 6], P(None, 'dp'), may hold values from -1.25 to 1.25
- up_bias: bfloat16 [2, 3072], P(None, 'dp'), may hold values from -1.25 to 1.25
- position_table: bfloat16 [768, 64], P('dp'), may hold values from -3 to 3
Outputs:
- layer_out: bfloat16 [2, 16, 2048, 768], P(None, 'dp', 'seg')
- input_grad: float32 [2, 16, 2048, 768], P(None, 'dp', 'seg')
- project_in_grad: float32 [2, 768, 2304], P(None, 'dp', 'seg')
- project_out_grad: float32 [2, 768, 768], P(None, 'dp', 'seg')
- up_weight_grad: float32 [2, 768, 3072], P(None, 'dp', 'seg')
- down_weight_grad: float32 [2, 3072, 768], P(None, 'dp', 'seg')
- norm_gains_grad: float32 [2, 768, 2], P(None, 'dp')
- biases_grad: float32 [2, 768, 6], P(None, 'dp')
- up_bias_grad: float32 [2, 3072], P(None, 'dp')
- position_table_grad: float32 [768, 64], P('dp')
Inputs may be any that keep to these rules, and one draw needn't show every extreme that they name: `document_ids`: document ids count from 0 in every row and never fall along it; a document has 1 to 8 segments.
All inputs are finite; a program needn't handle non-finite values.
Results may differ from a plain program's by a relative error of at most 0.028.
Values may be sent and summed in bfloat16 or wider, within the bound.
A program may use at most 320 MiB of HBM per device.

v0:
```python
import jax
import jax.numpy as jnp
from jax import lax
from jax.sharding import PartitionSpec as P

HEADS = 12
HD = 64
SEGLEN = 128
POS = 64
NORM_EPS = 1e-05
PRECISE = lax.Precision.HIGHEST


def norm_apply(inputs, norm_gain, norm_shift):
    average = jnp.mean(inputs, axis=-1, keepdims=True)
    centered = inputs - average
    variance = jnp.mean(centered * centered, axis=-1, keepdims=True)
    return centered * lax.rsqrt(variance + NORM_EPS) * norm_gain + norm_shift


def norm_backward(inputs, norm_gain, norm_shift, upstream):
    unused_out, pull_back = jax.vjp(norm_apply, inputs, norm_gain, norm_shift)
    return pull_back(upstream)


def gelu_exact(inputs):
    return jax.nn.gelu(inputs, approximate=False)


def soft_scores(queries, key_rows, same_document):
    scores = jnp.einsum(
        "gqhe,gkhe->ghqk", queries, key_rows, preferred_element_type=jnp.float32
    ) * HD ** (-0.5)
    if same_document is not None:
        scores = jnp.where(same_document[:, None, :, :], scores, -1e30)
    return scores


def block_forward(source, residual, weights, same_document):
    project_in, project_out, up_weight, down_weight, norm_gains, biases, up_bias = weights
    features = source.shape[-1]
    leading = source.shape[:-1]
    head_shape = leading + (HEADS, HD)
    joined = jnp.einsum("gld,de->gle", source, project_in, preferred_element_type=jnp.float32)
    queries = (joined[..., :features] + biases[:, 0]).astype(jnp.bfloat16)
    key_rows = joined[..., features : 2 * features].astype(jnp.bfloat16)
    values = (joined[..., 2 * features :] + biases[:, 1]).astype(jnp.bfloat16)
    scores = soft_scores(queries.reshape(head_shape), key_rows.reshape(head_shape), same_document)
    log_total = jax.nn.logsumexp(scores, axis=-1, keepdims=True)
    attention = jnp.exp(scores - log_total).astype(jnp.bfloat16)
    context = jnp.einsum(
        "ghqk,gkhe->gqhe", attention, values.reshape(head_shape), preferred_element_type=jnp.float32
    )
    context = context.reshape(leading + (features,)).astype(jnp.bfloat16)
    mixed_input = residual + (
        jnp.einsum("gld,de->gle", context, project_out, preferred_element_type=jnp.float32)
        + biases[:, 2]
    )
    first_norm = norm_apply(mixed_input, norm_gains[:, 0], biases[:, 4])
    first_low = first_norm.astype(jnp.bfloat16)
    pre_gelu = (
        jnp.einsum("gld,df->glf", first_low, up_weight, preferred_element_type=jnp.float32)
        + up_bias
    )
    activation = gelu_exact(pre_gelu).astype(jnp.bfloat16)
    second_input = first_norm + (
        jnp.einsum("glf,fd->gld", activation, down_weight, preferred_element_type=jnp.float32)
        + biases[:, 3]
    )
    result = norm_apply(second_input, norm_gains[:, 1], biases[:, 5])
    stored = (
        queries,
        key_rows,
        values,
        log_total,
        context,
        mixed_input,
        first_low,
        pre_gelu,
        activation,
        second_input,
    )
    return (result, stored)


def block_backward(source, stored, weights, same_document, upstream):
    project_in, project_out, up_weight, down_weight, norm_gains, biases, up_bias = weights
    (
        queries,
        key_rows,
        values,
        log_total,
        context,
        mixed_input,
        first_low,
        pre_gelu,
        activation,
        second_input,
    ) = stored
    features = source.shape[-1]
    leading = source.shape[:-1]
    head_shape = leading + (HEADS, HD)
    sum_axes = (0, 1)
    second_grad, gain_two, shift_two = norm_backward(
        second_input, norm_gains[:, 1], biases[:, 5], upstream
    )
    branch_grad = second_grad.astype(jnp.bfloat16)
    down_grad = jnp.einsum(
        "glf,gld->fd", activation, branch_grad, preferred_element_type=jnp.float32
    )
    activation_grad = jnp.einsum(
        "gld,fd->glf", branch_grad, down_weight, preferred_element_type=jnp.float32
    )
    unused_out, gelu_pull = jax.vjp(gelu_exact, pre_gelu)
    pre_gelu_grad = gelu_pull(activation_grad)[0].astype(jnp.bfloat16)
    up_grad = jnp.einsum(
        "gld,glf->df", first_low, pre_gelu_grad, preferred_element_type=jnp.float32
    )
    first_grad = second_grad + jnp.einsum(
        "glf,df->gld", pre_gelu_grad, up_weight, preferred_element_type=jnp.float32
    )
    mixed_grad, gain_one, shift_one = norm_backward(
        mixed_input, norm_gains[:, 0], biases[:, 4], first_grad
    )
    mixed_low = mixed_grad.astype(jnp.bfloat16)
    outward_grad = jnp.einsum("gld,gle->de", context, mixed_low, preferred_element_type=jnp.float32)
    context_grad = jnp.einsum(
        "gle,de->gld", mixed_low, project_out, preferred_element_type=jnp.float32
    )
    context_grad = context_grad.astype(jnp.bfloat16).reshape(head_shape)
    query_heads = queries.reshape(head_shape)
    key_heads = key_rows.reshape(head_shape)
    scores = soft_scores(query_heads, key_heads, same_document)
    attention = jnp.exp(scores - log_total)
    value_grad = jnp.einsum(
        "ghqk,gqhe->gkhe",
        attention.astype(jnp.bfloat16),
        context_grad,
        preferred_element_type=jnp.float32,
    )
    soft_grad = jnp.einsum(
        "gqhe,gkhe->ghqk",
        context_grad,
        values.reshape(head_shape),
        preferred_element_type=jnp.float32,
    )
    score_grad = attention * (soft_grad - jnp.sum(soft_grad * attention, axis=-1, keepdims=True))
    score_grad = score_grad.astype(jnp.bfloat16)
    query_grad = jnp.einsum(
        "ghqk,gkhe->gqhe", score_grad, key_heads, preferred_element_type=jnp.float32
    ) * HD ** (-0.5)
    key_grad = jnp.einsum(
        "ghqk,gqhe->gkhe", score_grad, query_heads, preferred_element_type=jnp.float32
    ) * HD ** (-0.5)
    joined_grad = jnp.concatenate(
        [
            query_grad.reshape(leading + (features,)),
            key_grad.reshape(leading + (features,)),
            value_grad.reshape(leading + (features,)),
        ],
        axis=-1,
    ).astype(jnp.bfloat16)
    inward_grad = jnp.einsum("gld,gle->de", source, joined_grad, preferred_element_type=jnp.float32)
    source_grad = mixed_grad + jnp.einsum(
        "gle,de->gld", joined_grad, project_in, preferred_element_type=jnp.float32
    )
    bias_grad = jnp.stack(
        [
            jnp.sum(joined_grad[..., :features], axis=sum_axes, dtype=jnp.float32),
            jnp.sum(joined_grad[..., 2 * features :], axis=sum_axes, dtype=jnp.float32),
            jnp.sum(mixed_low, axis=sum_axes, dtype=jnp.float32),
            jnp.sum(branch_grad, axis=sum_axes, dtype=jnp.float32),
            shift_one,
            shift_two,
        ],
        axis=-1,
    )
    gain_grad = jnp.stack([gain_one, gain_two], axis=-1)
    bias_up_grad = jnp.sum(pre_gelu_grad, axis=sum_axes, dtype=jnp.float32)
    return (
        source_grad,
        (inward_grad, outward_grad, up_grad, down_grad, gain_grad, bias_grad, bias_up_grad),
    )


def pick_block(weights, which_block):
    return (
        weights[0][which_block],
        weights[1][which_block],
        weights[2][which_block],
        weights[3][which_block],
        weights[4][which_block].astype(jnp.float32),
        weights[5][which_block].astype(jnp.float32),
        weights[6][which_block].astype(jnp.float32),
    )


def shards(
    tokens,
    cotangent,
    document_ids,
    position_ids,
    project_in,
    project_out,
    up_weight,
    down_weight,
    norm_gains,
    biases,
    up_bias,
    position_table,
):
    shard_index = lax.axis_index("seg")
    first_shard = (shard_index == 0).astype(jnp.float32)
    micro_count, row_count, row_tokens, features = tokens.shape
    segment_count = row_tokens // SEGLEN
    group_count = row_count * segment_count
    slot_ids = jnp.arange(POS, dtype=jnp.int32)
    outputs = []
    input_grads = []
    totals = None
    for micro_step in range(micro_count):
        weights = (
            lax.all_gather(
                lax.all_gather(project_in, "seg", axis=2, tiled=True), "dp", axis=1, tiled=True
            ),
            lax.all_gather(
                lax.all_gather(project_out, "seg", axis=2, tiled=True), "dp", axis=1, tiled=True
            ),
            lax.all_gather(
                lax.all_gather(up_weight, "seg", axis=2, tiled=True), "dp", axis=1, tiled=True
            ),
            lax.all_gather(
                lax.all_gather(down_weight, "seg", axis=2, tiled=True), "dp", axis=1, tiled=True
            ),
            lax.all_gather(norm_gains, "dp", axis=1, tiled=True),
            lax.all_gather(biases, "dp", axis=1, tiled=True),
            lax.all_gather(up_bias, "dp", axis=1, tiled=True),
            lax.all_gather(position_table, "dp", axis=0, tiled=True),
        )
        local_weights = pick_block(weights, 0)
        cross_weights = pick_block(weights, 1)
        gathered_table = weights[7]
        segments = tokens[micro_step].reshape(group_count, SEGLEN, features)
        local_out, local_stored = block_forward(
            segments, segments.astype(jnp.float32), local_weights, None
        )
        class_own = (
            local_out[:, 0, :].astype(jnp.bfloat16).reshape(row_count, segment_count, features)
        )
        class_rows = lax.all_gather(class_own, "seg", axis=1, tiled=True)
        one_hot = (position_ids[micro_step][:, :, None] == slot_ids).astype(jnp.bfloat16)
        cross_in = class_rows.astype(jnp.float32) + jnp.einsum(
            "rsp,dp->rsd", one_hot, gathered_table, preferred_element_type=jnp.float32
        )
        documents = document_ids[micro_step]
        same_document = documents[:, :, None] == documents[:, None, :]
        cross_low = cross_in.astype(jnp.bfloat16)
        cross_out, cross_stored = block_forward(cross_low, cross_in, cross_weights, same_document)
        cross_own = lax.dynamic_slice_in_dim(
            cross_out, shard_index * segment_count, segment_count, 1
        )
        merged = local_out.at[:, 0, :].set(cross_own.reshape(group_count, features))
        outputs.append(merged.astype(jnp.bfloat16).reshape(row_count, row_tokens, features))
        weights = (
            lax.all_gather(
                lax.all_gather(project_in, "seg", axis=2, tiled=True), "dp", axis=1, tiled=True
            ),
            lax.all_gather(
                lax.all_gather(project_out, "seg", axis=2, tiled=True), "dp", axis=1, tiled=True
            ),
            lax.all_gather(
                lax.all_gather(up_weight, "seg", axis=2, tiled=True), "dp", axis=1, tiled=True
            ),
            lax.all_gather(
                lax.all_gather(down_weight, "seg", axis=2, tiled=True), "dp", axis=1, tiled=True
            ),
            lax.all_gather(norm_gains, "dp", axis=1, tiled=True),
            lax.all_gather(biases, "dp", axis=1, tiled=True),
            lax.all_gather(up_bias, "dp", axis=1, tiled=True),
            lax.all_gather(position_table, "dp", axis=0, tiled=True),
        )
        local_weights = pick_block(weights, 0)
        cross_weights = pick_block(weights, 1)
        upstream = cotangent[micro_step].reshape(group_count, SEGLEN, features)
        class_grad_own = upstream[:, 0, :].reshape(row_count, segment_count, features)
        class_grads = lax.all_gather(class_grad_own, "seg", axis=1, tiled=True)
        cross_grad, cross_terms = block_backward(
            cross_low, cross_stored, cross_weights, same_document, class_grads.astype(jnp.float32)
        )
        table_grad = jnp.einsum(
            "rsd,rsp->dp", cross_grad, one_hot.astype(jnp.float32), precision=PRECISE
        )
        own_grad = lax.dynamic_slice_in_dim(
            cross_grad, shard_index * segment_count, segment_count, 1
        )
        local_upstream = (
            upstream.astype(jnp.float32).at[:, 0, :].set(own_grad.reshape(group_count, features))
        )
        token_grad, local_terms = block_backward(
            segments, local_stored, local_weights, None, local_upstream
        )
        input_grads.append(token_grad.reshape(row_count, row_tokens, features))
        gradients = tuple(
            (
                jnp.stack([local_term, cross_term * first_shard])
                for local_term, cross_term in zip(local_terms, cross_terms)
            )
        ) + (table_grad * first_shard,)
        small_sums = lax.psum(
            (
                lax.psum_scatter(
                    gradients[4].astype(jnp.bfloat16), "dp", scatter_dimension=1, tiled=True
                ).astype(jnp.float32),
                lax.psum_scatter(
                    gradients[5].astype(jnp.bfloat16), "dp", scatter_dimension=1, tiled=True
                ).astype(jnp.float32),
                lax.psum_scatter(
                    gradients[6].astype(jnp.bfloat16), "dp", scatter_dimension=1, tiled=True
                ).astype(jnp.float32),
                lax.psum_scatter(
                    gradients[7].astype(jnp.bfloat16), "dp", scatter_dimension=0, tiled=True
                ).astype(jnp.float32),
            ),
            "seg",
        )
        reduced = (
            lax.psum_scatter(
                lax.psum_scatter(
                    gradients[0].astype(jnp.bfloat16), "dp", scatter_dimension=1, tiled=True
                ),
                "seg",
                scatter_dimension=2,
                tiled=True,
            ).astype(jnp.float32),
            lax.psum_scatter(
                lax.psum_scatter(
                    gradients[1].astype(jnp.bfloat16), "dp", scatter_dimension=1, tiled=True
                ),
                "seg",
                scatter_dimension=2,
                tiled=True,
            ).astype(jnp.float32),
            lax.psum_scatter(
                lax.psum_scatter(
                    gradients[2].astype(jnp.bfloat16), "dp", scatter_dimension=1, tiled=True
                ),
                "seg",
                scatter_dimension=2,
                tiled=True,
            ).astype(jnp.float32),
            lax.psum_scatter(
                lax.psum_scatter(
                    gradients[3].astype(jnp.bfloat16), "dp", scatter_dimension=1, tiled=True
                ),
                "seg",
                scatter_dimension=2,
                tiled=True,
            ).astype(jnp.float32),
            small_sums[0],
            small_sums[1],
            small_sums[2],
            small_sums[3],
        )
        totals = (
            reduced
            if totals is None
            else tuple((jnp.add(earlier, current) for earlier, current in zip(totals, reduced)))
        )
    return (
        jnp.stack(outputs),
        jnp.stack(input_grads),
        totals[0],
        totals[1],
        totals[2],
        totals[3],
        totals[4],
        totals[5],
        totals[6],
        totals[7],
    )


def solution(mesh):
    placed = (
        P(None, "dp", "seg", None),
        P(None, "dp", "seg", None),
        P(None, "dp", None),
        P(None, "dp", None),
        P(None, "dp", "seg"),
        P(None, "dp", "seg"),
        P(None, "dp", "seg"),
        P(None, "dp", "seg"),
        P(None, "dp", None),
        P(None, "dp", None),
        P(None, "dp"),
        P("dp", None),
    )
    return jax.shard_map(
        shards,
        mesh=mesh,
        in_specs=placed,
        out_specs=(
            P(None, "dp", "seg", None),
            P(None, "dp", "seg", None),
            P(None, "dp", "seg"),
            P(None, "dp", "seg"),
            P(None, "dp", "seg"),
            P(None, "dp", "seg"),
            P(None, "dp", None),
            P(None, "dp", None),
            P(None, "dp"),
            P("dp", None),
        ),
        check_vma=False,
    )
```

profile of v0, /device:TPU:0, one launch (start us, length us, event | category | flops | bytes accessed | tf_op | source)
XLA Modules:
  0.0 1764.4 jit_solution(14379314771954475680)
XLA Ops:
  11.2 41.5 %all_gather.32 = bf16[2,96,2304]{1,0,2:T(2,128)(2,1)S(1)} all-gather(bf16[2,96,576]{1,0,2:T(2,128)(2,1)S(1)} %copy.324), channel_id=1, replica_groups=mesh['dp'=8,'seg'=4] {'seg'}, dimensions={2}, use_global_device_ids=true | all-gather | bytes 1105920 | tf_op jit(solution)/shard_map/all_gather | solution.py:224
  244.1 19.6 %fusion.38 = (u8[128,3072]{1,0:T(8,128)(4,1)S(1)}, u8[128,3072]{1,0:T(8,128)(4,1)S(1)}, u8[128,3072]{1,0:T(8,128)(4,1)S(1)}, u8[128,3072]{1,0:T(8,128)(4,1)S(1)}, f32[8,128,3072]{2,1,0:T(8,128)}) fusion(f32[3072]{0:T(1024)S(1)} %bitcast.509, f32[8,128,3072]{2,1,0:T(8,128)} %fusion.42, bf16[2,768,3072]{2,1,0:T(8,128)(2,1)} %all-gather.14.cloned.1.call-done, ...), kind=kOutput, calls=%fused_computation.141 | convolution fusion | flops 4922277888 | bytes 34629632 | tf_op jit(solution)/shard_map/gld,df->glf/dot_general | solution.py:62
  263.7 61.2 %multiply_convert_fusion.1 = (bf16[8,128,3072]{2,1,0:T(8,128)(2,1)}, f32[8,128,3072]{2,1,0:T(8,128)}, bf16[8,128,3072]{2,1,0:T(8,128)(2,1)}, f32[8,128,3072]{2,1,0:T(8,128)}) fusion(f32[8,128,3072]{2,1,0:T(8,128)} %get-tuple-element.267, f32[3072]{0:T(1024)S(1)} %bitcast.510, u8[128,3072]{1,0:T(8,128)(4,1)S(1)} %get-tuple-element.109, ...), kind=kLoop, calls=%fused_computation.28 | loop fusion | flops 443547648 | bytes 64499712 | tf_op jit(solution)/shard_map/convert_element_type | solution.py:65
  800.4 74.9 %all-reduce.10.cloned.1.call-done = (bf16[2,768,2304]{2,0,1:T(2,128)(2,1)}, bf16[2,768,2304]{2,0,1:T(2,128)(2,1)}) async-done(((bf16[2,768,2304]{2,0,1:T(2,128)(2,1)}, bf16[2,768,2304]{2,0,1:T(2,128)(2,1)}), (bf16[2,768,2304]{2,0,1:T(2,128)(2,1)}, bf16[2,768,2304]{2,0,1:T(2,128)(2,1)})) %all-reduce.10.cloned.1.call-update) | async-done | bytes 14155792
  877.1 47.8 %copy.434 = bf16[2,96,2304]{0,1,2:T(8,128)(2,1)} copy(bf16[2,96,2304]{2,0,1:T(2,128)(2,1)S(1)} %constant_dynamic-slice_fusion.1) | data formatting | bytes 1769472
  924.8 83.7 %reshape.972 = bf16[2304,192]{1,0:T(8,128)(2,1)} reshape(bf16[2304,96,2]{2,1,0:T(8,128)(2,1)} %bitcast.442) | data formatting | bytes 1769472
  1010.4 47.8 %copy.436 = bf16[2,96,2304]{0,1,2:T(8,128)(2,1)} copy(bf16[2,96,2304]{2,0,1:T(2,128)(2,1)S(1)} %constant_dynamic-slice_fusion) | data formatting | bytes 1769472
  1058.2 83.7 %reshape.974 = bf16[2304,192]{1,0:T(8,128)(2,1)} reshape(bf16[2304,96,2]{2,1,0:T(8,128)(2,1)} %bitcast.443) | data formatting | bytes 1769472
  1164.1 31.9 %reduce-scatter.49.cloned.1.call-done = bf16[2,96,3072]{2,1,0:T(8,128)(2,1)} async-done(((bf16[2,768,3072]{2,1,0:T(8,128)(2,1)}), bf16[2,96,3072]{2,1,0:T(8,128)(2,1)}) %reduce-scatter.49.cloned.1.call-update) | async-done | bytes 1179664 | tf_op jit(solution)/shard_map/reduce_scatter | solution.py:344
  1234.1 36.2 %reduce-scatter.69.cloned.1.call-done = bf16[96,4]{1,0:T(8,128)(2,1)} async-done(((bf16[768,4]{1,0:T(8,128)(2,1)}), bf16[96,4]{1,0:T(8,128)(2,1)}) %reduce-scatter.69.cloned.1.call-update) | async-done | bytes 784
  1271.2 37.0 %reduce-scatter.79.cloned.1.call-done = bf16[384,2]{1,0:T(8,128)(2,1)} async-done(((bf16[3072,2]{1,0:T(8,128)(2,1)}), bf16[384,2]{1,0:T(8,128)(2,1)}) %reduce-scatter.79.cloned.1.call-update) | async-done | bytes 1552
  1309.2 37.0 %reduce-scatter.77.cloned.1.call-done = bf16[384,2]{1,0:T(8,128)(2,1)} async-done(((bf16[3072,2]{1,0:T(8,128)(2,1)}), bf16[384,2]{1,0:T(8,128)(2,1)}) %reduce-scatter.77.cloned.1.call-update) | async-done | bytes 1552
  1347.2 35.6 %reduce-scatter.75.cloned.1.call-done = bf16[96,12]{1,0:T(8,128)(2,1)} async-done(((bf16[768,12]{1,0:T(8,128)(2,1)}), bf16[96,12]{1,0:T(8,128)(2,1)}) %reduce-scatter.75.cloned.1.call-update) | async-done | bytes 2320
  1383.8 35.8 %reduce-scatter.73.cloned.1.call-done = bf16[96,12]{1,0:T(8,128)(2,1)} async-done(((bf16[768,12]{1,0:T(8,128)(2,1)}), bf16[96,12]{1,0:T(8,128)(2,1)}) %reduce-scatter.73.cloned.1.call-update) | async-done | bytes 2320
  1420.4 35.6 %reduce-scatter.81.cloned.1.call-done = bf16[96,64]{1,0:T(8,128)(2,1)} async-done(((bf16[768,64]{1,0:T(8,128)(2,1)}), bf16[96,64]{1,0:T(8,128)(2,1)}) %reduce-scatter.81.cloned.1.call-update) | async-done | bytes 12304
  1456.9 35.9 %reduce-scatter.83.cloned.1.call-done = bf16[96,64]{1,0:T(8,128)(2,1)} async-done(((bf16[768,64]{1,0:T(8,128)(2,1)}), bf16[96,64]{1,0:T(8,128)(2,1)}) %reduce-scatter.83.cloned.1.call-update) | async-done | bytes 12304
  1493.6 20.4 %all-reduce.4 = (f32[2,96,2]{1,2,0:T(2,128)}, f32[2,96,6]{1,2,0:T(8,128)S(1)}, f32[2,384]{1,0:T(2,128)}, f32[96,64]{0,1:T(8,128)}) all-reduce(f32[2,96,2]{1,2,0:T(2,128)S(1)} %convert_add_fusion.7, f32[2,96,6]{1,2,0:T(8,128)S(1)} %convert_add_fusion.5, f32[2,384]{1,0:T(2,128)S(1)} %convert_add_fusion.6, ...), channel_id=1, replica_groups=mesh['dp'=8,'seg'=4] {'seg'}, use_global_device_ids=true, to_apply=%region_65.66 | all-reduce | flops 8448 | bytes 67584 | tf_op jit(solution)/shard_map/psum | solution.py:309
  1517.8 20.9 %reduce-scatter.65.cloned.1.call-done = bf16[192,192]{1,0:T(8,128)(2,1)} async-done(((bf16[768,192]{1,0:T(8,128)(2,1)}), bf16[192,192]{1,0:T(8,128)(2,1)}) %reduce-scatter.65.cloned.1.call-update) | async-done | bytes 73744
  1540.6 27.9 %reduce-scatter.61.cloned.1.call-done = bf16[576,192]{1,0:T(8,128)(2,1)} async-done(((bf16[2304,192]{1,0:T(8,128)(2,1)}), bf16[576,192]{1,0:T(8,128)(2,1)}) %reduce-scatter.61.cloned.1.call-update) | async-done | bytes 221200
  1568.5 31.4 %reshape.973 = bf16[576,96,2]{2,1,0:T(8,128)(2,1)} reshape(bf16[576,192]{1,0:T(8,128)(2,1)} %reduce-scatter.61.cloned.1.call-done) | data formatting | bytes 442368
  1614.6 31.4 %reshape.975 = bf16[576,96,2]{2,1,0:T(8,128)(2,1)} reshape(bf16[576,192]{1,0:T(8,128)(2,1)} %reduce-scatter.63.cloned.1.call-done) | data formatting | bytes 442368
  1661.4 32.9 %all-reduce.12.cloned.1.call-done = (bf16[2,384,768]{1,0,2:T(2,128)(2,1)}, bf16[2,384,768]{1,0,2:T(2,128)(2,1)}) async-done(((bf16[2,384,768]{1,0,2:T(2,128)(2,1)}, bf16[2,384,768]{1,0,2:T(2,128)(2,1)}), (bf16[2,384,768]{1,0,2:T(2,128)(2,1)}, bf16[2,384,768]{1,0,2:T(2,128)(2,1)})) %all-reduce.12.cloned.1.call-update) | async-done | bytes 2359312
  1696.6 28.4 %reduce-scatter.55.cloned.1.call-done = bf16[2,96,768]{2,1,0:T(8,128)(2,1)} async-done(((bf16[2,96,3072]{2,1,0:T(8,128)(2,1)}), bf16[2,96,768]{2,1,0:T(8,128)(2,1)}) %reduce-scatter.55.cloned.1.call-update) | async-done | bytes 294928 | tf_op jit(solution)/shard_map/reduce_scatter | solution.py:343
  1724.9 30.3 %reduce-scatter.51.cloned.1.call-done = bf16[2,96,768]{2,1,0:T(8,128)(2,1)} async-done(((bf16[2,96,3072]{2,1,0:T(8,128)(2,1)}), bf16[2,96,768]{2,1,0:T(8,128)(2,1)}) %reduce-scatter.51.cloned.1.call-update) | async-done | bytes 294928 | tf_op jit(solution)/shard_map/reduce_scatter | solution.py:343
  (907 shorter events, 775.9 us)
Async XLA Ops:
  73.0 159.9 %all-gather.14.cloned.1.call-start = ((), (), s32[]{:S(2)}) async-start(), calls=%async_computation.23 | async-start | bytes 10616832 | tf_op jit(solution)/shard_map/all_gather | solution.py:229
  73.6 251.4 %all-gather.18.cloned.1.call-start = ((), (), s32[]{:S(2)}) async-start(), calls=%async_computation.25 | async-start | bytes 10616832 | tf_op jit(solution)/shard_map/all_gather | solution.py:232
  158.9 635.3 %reduce-scatter.47.cloned.1.call-start = ((), (), s32[]{:S(2)}) async-start(), calls=%async_computation.27 | async-start | bytes 2654208 | tf_op jit(solution)/shard_map/reduce_scatter | solution.py:336
  563.9 232.9 %reduce-scatter.45.cloned.1.call-start = ((), (), s32[]{:S(2)}) async-start(), calls=%async_computation.26 | async-start | bytes 2654208 | tf_op jit(solution)/shard_map/reduce_scatter | solution.py:336
  618.4 256.9 %all-reduce.10.cloned.1.call-start = ((), (), s32[]{:S(2)}) async-start(), calls=%async_computation.46 | async-start | bytes 28311552
  685.8 456.2 %reduce-scatter.59.cloned.1.call-start = ((), (), s32[]{:S(2)}) async-start(), calls=%async_computation.33 | async-start | bytes 10616832 | tf_op jit(solution)/shard_map/reduce_scatter | solution.py:352
  710.4 436.5 %reduce-scatter.57.cloned.1.call-start = ((), (), s32[]{:S(2)}) async-start(), calls=%async_computation.32 | async-start | bytes 10616832 | tf_op jit(solution)/shard_map/reduce_scatter | solution.py:352
  734.4 417.3 %reduce-scatter.53.cloned.1.call-start = ((), (), s32[]{:S(2)}) async-start(), calls=%async_computation.30 | async-start | bytes 10616832 | tf_op jit(solution)/shard_map/reduce_scatter | solution.py:344
  758.1 437.9 %reduce-scatter.49.cloned.1.call-start = ((), (), s32[]{:S(2)}) async-start(), calls=%async_computation.28 | async-start | bytes 10616832 | tf_op jit(solution)/shard_map/reduce_scatter | solution.py:344
  781.5 451.6 %reduce-scatter.71.cloned.1.call-start = ((), (), s32[]{:S(2)}) async-start(), calls=%async_computation.39 | async-start | bytes 221184
  783.9 486.4 %reduce-scatter.69.cloned.1.call-start = ((), (), s32[]{:S(2)}) async-start(), calls=%async_computation.38 | async-start | bytes 221184
  785.3 522.9 %reduce-scatter.79.cloned.1.call-start = ((), (), s32[]{:S(2)}) async-start(), calls=%async_computation.43 | async-start | bytes 884736
  786.8 559.4 %reduce-scatter.77.cloned.1.call-start = ((), (), s32[]{:S(2)}) async-start(), calls=%async_computation.42 | async-start | bytes 884736
  788.5 594.4 %reduce-scatter.75.cloned.1.call-start = ((), (), s32[]{:S(2)}) async-start(), calls=%async_computation.41 | async-start | bytes 221184
  790.2 629.3 %reduce-scatter.73.cloned.1.call-start = ((), (), s32[]{:S(2)}) async-start(), calls=%async_computation.40 | async-start | bytes 221184
  791.6 664.4 %reduce-scatter.81.cloned.1.call-start = ((), (), s32[]{:S(2)}) async-start(), calls=%async_computation.44 | async-start | bytes 221184
  792.9 699.8 %reduce-scatter.83.cloned.1.call-start = ((), (), s32[]{:S(2)}) async-start(), calls=%async_computation.45 | async-start | bytes 221184
  794.2 722.5 %reduce-scatter.67.cloned.1.call-start = ((), (), s32[]{:S(2)}) async-start(), calls=%async_computation.37 | async-start | bytes 491520
  796.8 742.0 %reduce-scatter.65.cloned.1.call-start = ((), (), s32[]{:S(2)}) async-start(), calls=%async_computation.36 | async-start | bytes 491520
  799.1 769.4 %reduce-scatter.61.cloned.1.call-start = ((), (), s32[]{:S(2)}) async-start(), calls=%async_computation.34 | async-start | bytes 1474560
  1008.6 606.0 %reduce-scatter.63.cloned.1.call-start = ((), (), s32[]{:S(2)}) async-start(), calls=%async_computation.35 | async-start | bytes 1474560
  1141.9 552.4 %all-reduce.12.cloned.1.call-start = ((), (), s32[]{:S(2)}) async-start(), calls=%async_computation.47 | async-start | bytes 4718592
  1151.6 573.3 %reduce-scatter.55.cloned.1.call-start = ((), (), s32[]{:S(2)}) async-start(), calls=%async_computation.31 | async-start | bytes 1474560 | tf_op jit(solution)/shard_map/reduce_scatter | solution.py:343
  1152.2 602.9 %reduce-scatter.51.cloned.1.call-start = ((), (), s32[]{:S(2)}) async-start(), calls=%async_computation.29 | async-start | bytes 1474560 | tf_op jit(solution)/shard_map/reduce_scatter | solution.py:343
  (235 other events, 3767.6 us)
Sparse Core Ops, SparseCore 0:
  9.6 46.6 all-gather.11
  58.4 31.0 all-gather.15
  91.9 49.1 all-gather.7
  143.5 28.8 all-gather.9
  174.1 58.6 all-gather.13
  234.6 58.6 all-gather.17
  564.0 42.2 reduce-scatter.46
  618.5 42.4 reduce-scatter.44
  685.9 189.3 all-reduce.9
  878.6 76.7 reduce-scatter.58
  959.0 76.6 reduce-scatter.56
  1039.1 76.6 reduce-scatter.52
  1119.3 76.6 reduce-scatter.48
  1199.5 33.6 reduce-scatter.70
  1236.6 33.6 reduce-scatter.68
  1273.3 34.9 reduce-scatter.78
  1311.3 34.9 reduce-scatter.76
  1349.1 33.6 reduce-scatter.74
  1385.9 33.6 reduce-scatter.72
  1422.4 33.6 reduce-scatter.80
  1459.1 33.6 reduce-scatter.82
  1570.8 27.9 reduce-scatter.62
  1601.0 93.2 all-reduce.11
  1696.5 28.3 reduce-scatter.54
  (4 shorter events, 95.5 us)
where the time goes:
time: 1770 us; the launch traced here: 1760 us
  local copies, waits for them, and re-layouts  541 us (31%)
  waiting for transfers between devices  534 us (30%)
  matrix products  322 us (18%)
  other arithmetic  175 us (10%)
  blocking collectives  171 us (10%)
  between operations  19.8 us (1%)
    unnamed x42, waiting for transfers between devices  430 us
    unnamed x521, local copies, waits for them, and re-layouts  424 us
    convert_element_type x1, other arithmetic, block_forward(): activation = gelu_exact(pre_gelu).astype(jnp.bfloat16)  61.2 us
    reduce_scatter x2, waiting for transfers between devices, shards(): lax.psum_scatter(lax.psum_scatter(gradients[2].astype(jnp.bfloat16), 'dp'...  58.6 us
    another operation x16, other arithmetic, shards(): jnp.stack([local_term, cross_term * first_shard])  44.5 us
    all_gather x1, blocking collectives, shards(): lax.all_gather(project_in, 'seg', axis=2, tiled=True)  41.5 us
    dot_general x4, matrix products, block_backward(): jnp.einsum('gld,fd->glf', branch_grad, down_weight, preferred_element_typ...  41.3 us
    another operation x4, local copies, waits for them, and re-layouts, shards(): jnp.stack([local_term, cross_term * first_shard])  36.7 us
  transfers between devices with their start and end apart: 28, of which 17 were waited for; matrix products, arithmetic and copies ran while one was open for 45% of the time, Pallas kernels for 0%

commit v1 on v0

--- a/solution.py
+++ b/solution.py
@@ -9,6 +9,33 @@
 POS = 64
 NORM_EPS = 1e-05
 PRECISE = lax.Precision.HIGHEST
+
+
+def waves_draft(x0, axis_key, where_dim):
+    z_new = lax.axis_size(axis_key)
+    aux = lax.axis_index(axis_key)
+    current_block, y, part_now = (z_new, aux, x0.shape[where_dim])
+    entries = tuple(((rr, (rr + 1) % current_block) for rr in range(current_block)))
+    heap = tuple(((rr, (rr - 1) % current_block) for rr in range(current_block)))
+    tmp = jnp.zeros(
+        (*x0.shape[:where_dim], current_block * part_now, *x0.shape[where_dim + 1 :]), x0.dtype
+    )
+    tmp = lax.dynamic_update_slice_in_dim(tmp, x0, y * part_now, axis=where_dim)
+    odd = lower = x0
+    fresh = current_block // 2
+    num = 1
+    while num < fresh + 1:
+        odd = lax.ppermute(odd, axis_key, perm=entries)
+        tmp = lax.dynamic_update_slice_in_dim(
+            tmp, odd, (y - num) % current_block * part_now, axis=where_dim
+        )
+        if num < current_block - fresh:
+            lower = lax.ppermute(lower, axis_key, heap)
+            tmp = lax.dynamic_update_slice_in_dim(
+                tmp, lower, (y + num) % current_block * part_now, axis=where_dim
+            )
+        num += 1
+    return tmp
 
 
 def norm_apply(inputs, norm_gain, norm_shift):
@@ -220,9 +247,7 @@
     totals = None
     for micro_step in range(micro_count):
         weights = (
-            lax.all_gather(
-                lax.all_gather(project_in, "seg", axis=2, tiled=True), "dp", axis=1, tiled=True
-            ),
+            waves_draft(lax.all_gather(project_in, "seg", axis=2, tiled=True), "dp", 1),
             lax.all_gather(
                 lax.all_gather(project_out, "seg", axis=2, tiled=True), "dp", axis=1, tiled=True
             ),

time: 1770 us -> 1990 us (1.12)
  local copies, waits for them, and re-layouts: 541 us -> 681 us
  matrix products: 322 us -> 346 us
    dynamic_update_slice x0 -> x8, local copies, waits for them, and re-layouts: none -> 116 us  [the longest x4 57.8 us: waves_draft(): lax.dynamic_update_slice_in_dim(tmp, odd, (y - num) % current_block * par...]
    ppermute x0 -> x7, waiting for transfers between devices: none -> 24.8 us  [the longest x3 24 us: waves_draft(): lower = lax.ppermute(lower, axis_key, heap)]
    unnamed x521 -> x511, local copies, waits for them, and re-layouts: 424 us -> 407 us
  transfers between devices with their start and end apart: 28 -> 35, of which waited for: 17 -> 18; matrix products, arithmetic and copies ran while one was open for 45% -> 50% of each run, Pallas kernels for 0% -> 0%
where the time goes in v1:
time: 1990 us; the launch traced here: 1970 us
  local copies, waits for them, and re-layouts  681 us (34%)
  waiting for transfers between devices  540 us (27%)
  matrix products  346 us (17%)
  blocking collectives  190 us (10%)
  other arithmetic  181 us (9%)
    unnamed x42, waiting for transfers between devices  426 us
    unnamed x511, local copies, waits for them, and re-layouts  407 us
    convert_element_type x1, other arithmetic, block_forward(): activation = gelu_exact(pre_gelu).astype(jnp.bfloat16)  61.4 us
    reduce_scatter x2, waiting for transfers between devices, shards(): lax.psum_scatter(lax.psum_scatter(gradients[2].astype(jnp.bfloat16), 'dp'...  58.6 us
    dynamic_update_slice x4, local copies, waits for them, and re-layouts, waves_draft(): lax.dynamic_update_slice_in_dim(tmp, odd, (y - num) % current_block * par...  57.8 us
    dynamic_update_slice x3, local copies, waits for them, and re-layouts, waves_draft(): lax.dynamic_update_slice_in_dim(tmp, lower, (y + num) % current_block * p...  45.4 us
    another operation x16, other arithmetic, shards(): jnp.stack([local_term, cross_term * first_shard])  44.5 us
    dot_general x4, matrix products, block_backward(): jnp.einsum('gld,fd->glf', branch_grad, down_weight, preferred_element_typ...  41.7 us
  transfers between devices with their start and end apart: 35, of which 18 were waited for; matrix products, arithmetic and copies ran while one was open for 50% of the time, Pallas kernels for 0%

profile of v1, /device:TPU:0, one launch (start us, length us, event | category | flops | bytes accessed | tf_op | source)
XLA Modules:
  0.0 1968.3 jit_solution(17414852707030083559)
XLA Ops:
  32.7 31.8 %all_gather.32 = bf16[2,96,2304]{1,2,0:T(8,128)(2,1)S(1)} all-gather(bf16[2,96,576]{1,2,0:T(8,128)(2,1)S(1)} %copy.334), channel_id=1, replica_groups=mesh['dp'=8,'seg'=4] {'seg'}, dimensions={2}, use_global_device_ids=true | all-gather | bytes 1105920 | tf_op jit(solution)/shard_map/all_gather | solution.py:250
  71.1 24.3 %all_gather.33 = bf16[2,768,6]{2,0,1:T(2,128)(2,1)S(1)} all-gather(bf16[2,96,6]{2,0,1:T(2,128)(2,1)S(1)} %copy.344), channel_id=1, replica_groups=mesh['dp'=8,'seg'=4] {'dp'}, dimensions={1}, use_global_device_ids=true | all-gather | bytes 20736 | tf_op jit(solution)/shard_map/all_gather | solution.py:261
  197.2 24.0 %collective-permute-done.3 = bf16[2,96,2304]{2,1,0:T(8,128)(2,1)} collective-permute-done((bf16[2,96,2304]{2,1,0:T(8,128)(2,1)}, bf16[2,96,2304]{2,1,0:T(8,128)(2,1)}, u32[]{:S(2)}, u32[]{:S(2)}) %collective-permute-start.3) | collective-permute-done | bytes 884768 | tf_op jit(solution)/shard_map/ppermute | solution.py:33
  432.4 61.4 %multiply_convert_fusion.1 = (bf16[8,128,3072]{2,1,0:T(8,128)(2,1)}, f32[8,128,3072]{2,1,0:T(8,128)}, bf16[8,128,3072]{2,1,0:T(8,128)(2,1)}, f32[8,128,3072]{2,1,0:T(8,128)}) fusion(f32[8,128,3072]{2,1,0:T(8,128)} %get-tuple-element.269, f32[3072]{0:T(1024)S(1)} %bitcast.516, u8[128,3072]{1,0:T(8,128)(4,1)S(1)} %get-tuple-element.109, ...), kind=kLoop, calls=%fused_computation.28 | loop fusion | flops 443547648 | bytes 64499712 | tf_op jit(solution)/shard_map/convert_element_type | solution.py:92
  1007.0 72.6 %all-reduce.10.cloned.1.call-done = (bf16[2,768,2304]{2,0,1:T(2,128)(2,1)}, bf16[2,768,2304]{2,0,1:T(2,128)(2,1)}) async-done(((bf16[2,768,2304]{2,0,1:T(2,128)(2,1)}, bf16[2,768,2304]{2,0,1:T(2,128)(2,1)}), (bf16[2,768,2304]{2,0,1:T(2,128)(2,1)}, bf16[2,768,2304]{2,0,1:T(2,128)(2,1)})) %all-reduce.10.cloned.1.call-update) | async-done | bytes 14155792
  1081.4 47.8 %copy.457 = bf16[2,96,2304]{0,1,2:T(8,128)(2,1)} copy(bf16[2,96,2304]{2,0,1:T(2,128)(2,1)S(1)} %constant_dynamic-slice_fusion) | data formatting | bytes 1769472
  1129.2 83.7 %reshape.977 = bf16[2304,192]{1,0:T(8,128)(2,1)} reshape(bf16[2304,96,2]{2,1,0:T(8,128)(2,1)} %bitcast.450) | data formatting | bytes 1769472
  1214.8 47.8 %copy.455 = bf16[2,96,2304]{0,1,2:T(8,128)(2,1)} copy(bf16[2,96,2304]{2,0,1:T(2,128)(2,1)S(1)} %constant_dynamic-slice_fusion.1) | data formatting | bytes 1769472
  1262.5 83.7 %reshape.975 = bf16[2304,192]{1,0:T(8,128)(2,1)} reshape(bf16[2304,96,2]{2,1,0:T(8,128)(2,1)} %bitcast.451) | data formatting | bytes 1769472
  1369.6 30.7 %reduce-scatter.53.cloned.1.call-done = bf16[2,96,3072]{2,1,0:T(8,128)(2,1)} async-done(((bf16[2,768,3072]{2,1,0:T(8,128)(2,1)}), bf16[2,96,3072]{2,1,0:T(8,128)(2,1)}) %reduce-scatter.53.cloned.1.call-update) | async-done | bytes 1179664 | tf_op jit(solution)/shard_map/reduce_scatter | solution.py:369
  1438.3 36.2 %reduce-scatter.71.cloned.1.call-done = bf16[96,4]{1,0:T(8,128)(2,1)} async-done(((bf16[768,4]{1,0:T(8,128)(2,1)}), bf16[96,4]{1,0:T(8,128)(2,1)}) %reduce-scatter.71.cloned.1.call-update) | async-done | bytes 784
  1475.4 37.0 %reduce-scatter.77.cloned.1.call-done = bf16[384,2]{1,0:T(8,128)(2,1)} async-done(((bf16[3072,2]{1,0:T(8,128)(2,1)}), bf16[384,2]{1,0:T(8,128)(2,1)}) %reduce-scatter.77.cloned.1.call-update) | async-done | bytes 1552
  1513.5 37.0 %reduce-scatter.79.cloned.1.call-done = bf16[384,2]{1,0:T(8,128)(2,1)} async-done(((bf16[3072,2]{1,0:T(8,128)(2,1)}), bf16[384,2]{1,0:T(8,128)(2,1)}) %reduce-scatter.79.cloned.1.call-update) | async-done | bytes 1552
  1551.4 35.6 %reduce-scatter.73.cloned.1.call-done = bf16[96,12]{1,0:T(8,128)(2,1)} async-done(((bf16[768,12]{1,0:T(8,128)(2,1)}), bf16[96,12]{1,0:T(8,128)(2,1)}) %reduce-scatter.73.cloned.1.call-update) | async-done | bytes 2320
  1587.9 35.8 %reduce-scatter.75.cloned.1.call-done = bf16[96,12]{1,0:T(8,128)(2,1)} async-done(((bf16[768,12]{1,0:T(8,128)(2,1)}), bf16[96,12]{1,0:T(8,128)(2,1)}) %reduce-scatter.75.cloned.1.call-update) | async-done | bytes 2320
  1624.6 35.6 %reduce-scatter.83.cloned.1.call-done = bf16[96,64]{1,0:T(8,128)(2,1)} async-done(((bf16[768,64]{1,0:T(8,128)(2,1)}), bf16[96,64]{1,0:T(8,128)(2,1)}) %reduce-scatter.83.cloned.1.call-update) | async-done | bytes 12304
  1661.0 35.9 %reduce-scatter.81.cloned.1.call-done = bf16[96,64]{1,0:T(8,128)(2,1)} async-done(((bf16[768,64]{1,0:T(8,128)(2,1)}), bf16[96,64]{1,0:T(8,128)(2,1)}) %reduce-scatter.81.cloned.1.call-update) | async-done | bytes 12304
  1697.7 21.1 %all-reduce.4 = (f32[2,96,2]{1,2,0:T(2,128)}, f32[2,96,6]{1,2,0:T(8,128)S(1)}, f32[2,384]{1,0:T(2,128)}, f32[96,64]{0,1:T(8,128)}) all-reduce(f32[2,96,2]{1,2,0:T(2,128)S(1)} %convert_add_fusion.7, f32[2,96,6]{1,2,0:T(8,128)S(1)} %convert_add_fusion.5, f32[2,384]{1,0:T(2,128)S(1)} %convert_add_fusion.6, ...), channel_id=1, replica_groups=mesh['dp'=8,'seg'=4] {'seg'}, use_global_device_ids=true, to_apply=%region_65.66 | all-reduce | flops 8448 | bytes 67584 | tf_op jit(solution)/shard_map/psum | solution.py:334
  1744.4 28.0 %reduce-scatter.63.cloned.1.call-done = bf16[576,192]{1,0:T(8,128)(2,1)} async-done(((bf16[2304,192]{1,0:T(8,128)(2,1)}), bf16[576,192]{1,0:T(8,128)(2,1)}) %reduce-scatter.63.cloned.1.call-update) | async-done | bytes 221200
  1772.4 31.4 %reshape.978 = bf16[576,96,2]{2,1,0:T(8,128)(2,1)} reshape(bf16[576,192]{1,0:T(8,128)(2,1)} %reduce-scatter.63.cloned.1.call-done) | data formatting | bytes 442368
  1818.5 31.4 %reshape.976 = bf16[576,96,2]{2,1,0:T(8,128)(2,1)} reshape(bf16[576,192]{1,0:T(8,128)(2,1)} %reduce-scatter.61.cloned.1.call-done) | data formatting | bytes 442368
  1865.3 32.9 %all-reduce.12.cloned.1.call-done = (bf16[2,384,768]{1,0,2:T(2,128)(2,1)}, bf16[2,384,768]{1,0,2:T(2,128)(2,1)}) async-done(((bf16[2,384,768]{1,0,2:T(2,128)(2,1)}, bf16[2,384,768]{1,0,2:T(2,128)(2,1)}), (bf16[2,384,768]{1,0,2:T(2,128)(2,1)}, bf16[2,384,768]{1,0,2:T(2,128)(2,1)})) %all-reduce.12.cloned.1.call-update) | async-done | bytes 2359312
  1900.5 28.3 %reduce-scatter.51.cloned.1.call-done = bf16[2,96,768]{2,1,0:T(8,128)(2,1)} async-done(((bf16[2,96,3072]{2,1,0:T(8,128)(2,1)}), bf16[2,96,768]{2,1,0:T(8,128)(2,1)}) %reduce-scatter.51.cloned.1.call-update) | async-done | bytes 294928 | tf_op jit(solution)/shard_map/reduce_scatter | solution.py:368
  1928.8 30.3 %reduce-scatter.55.cloned.1.call-done = bf16[2,96,768]{2,1,0:T(8,128)(2,1)} async-done(((bf16[2,96,3072]{2,1,0:T(8,128)(2,1)}), bf16[2,96,768]{2,1,0:T(8,128)(2,1)}) %reduce-scatter.55.cloned.1.call-update) | async-done | bytes 294928 | tf_op jit(solution)/shard_map/reduce_scatter | solution.py:368
  (920 shorter events, 984.5 us)
Async XLA Ops:
  10.0 370.4 %all-gather.8.cloned.1.call-start = ((), (), s32[]{:S(2)}) async-start(), calls=%async_computation.20 | async-start | bytes 2654208 | tf_op jit(solution)/shard_map/all_gather | solution.py:251
  31.5 355.1 %all-gather.18.cloned.1.call-start = ((), (), s32[]{:S(2)}) async-start(), calls=%async_computation.25 | async-start | bytes 7962624 | tf_op jit(solution)/shard_map/all_gather | solution.py:290
  66.4 335.7 %all-gather.12.cloned.1.call-start = ((), (), s32[]{:S(2)}) async-start(), calls=%async_computation.22 | async-start | bytes 10616832 | tf_op jit(solution)/shard_map/all_gather | solution.py:254
  67.0 426.8 %all-gather.16.cloned.1.call-start = ((), (), s32[]{:S(2)}) async-start(), calls=%async_computation.24 | async-start | bytes 10616832 | tf_op jit(solution)/shard_map/all_gather | solution.py:257
  264.8 736.1 %reduce-scatter.45.cloned.1.call-start = ((), (), s32[]{:S(2)}) async-start(), calls=%async_computation.26 | async-start | bytes 2654208 | tf_op jit(solution)/shard_map/reduce_scatter | solution.py:361
  891.7 454.6 %reduce-scatter.57.cloned.1.call-start = ((), (), s32[]{:S(2)}) async-start(), calls=%async_computation.32 | async-start | bytes 10616832 | tf_op jit(solution)/shard_map/reduce_scatter | solution.py:377
  916.2 435.0 %reduce-scatter.59.cloned.1.call-start = ((), (), s32[]{:S(2)}) async-start(), calls=%async_computation.33 | async-start | bytes 10616832 | tf_op jit(solution)/shard_map/reduce_scatter | solution.py:377
  941.2 414.9 %reduce-scatter.49.cloned.1.call-start = ((), (), s32[]{:S(2)}) async-start(), calls=%async_computation.28 | async-start | bytes 10616832 | tf_op jit(solution)/shard_map/reduce_scatter | solution.py:369
  964.7 435.6 %reduce-scatter.53.cloned.1.call-start = ((), (), s32[]{:S(2)}) async-start(), calls=%async_computation.30 | async-start | bytes 10616832 | tf_op jit(solution)/shard_map/reduce_scatter | solution.py:369
  988.1 449.4 %reduce-scatter.69.cloned.1.call-start = ((), (), s32[]{:S(2)}) async-start(), calls=%async_computation.38 | async-start | bytes 221184
  990.3 484.3 %reduce-scatter.71.cloned.1.call-start = ((), (), s32[]{:S(2)}) async-start(), calls=%async_computation.39 | async-start | bytes 221184
  991.7 520.8 %reduce-scatter.77.cloned.1.call-start = ((), (), s32[]{:S(2)}) async-start(), calls=%async_computation.42 | async-start | bytes 884736
  993.1 557.3 %reduce-scatter.79.cloned.1.call-start = ((), (), s32[]{:S(2)}) async-start(), calls=%async_computation.43 | async-start | bytes 884736
  995.0 592.0 %reduce-scatter.73.cloned.1.call-start = ((), (), s32[]{:S(2)}) async-start(), calls=%async_computation.40 | async-start | bytes 221184
  996.8 626.8 %reduce-scatter.75.cloned.1.call-start = ((), (), s32[]{:S(2)}) async-start(), calls=%async_computation.41 | async-start | bytes 221184
  998.3 661.9 %reduce-scatter.83.cloned.1.call-start = ((), (), s32[]{:S(2)}) async-start(), calls=%async_computation.45 | async-start | bytes 221184
  999.6 697.3 %reduce-scatter.81.cloned.1.call-start = ((), (), s32[]{:S(2)}) async-start(), calls=%async_computation.44 | async-start | bytes 221184
  1000.8 720.2 %reduce-scatter.65.cloned.1.call-start = ((), (), s32[]{:S(2)}) async-start(), calls=%async_computation.36 | async-start | bytes 491520
  1003.2 739.4 %reduce-scatter.67.cloned.1.call-start = ((), (), s32[]{:S(2)}) async-start(), calls=%async_computation.37 | async-start | bytes 491520
  1005.5 766.9 %reduce-scatter.63.cloned.1.call-start = ((), (), s32[]{:S(2)}) async-start(), calls=%async_computation.35 | async-start | bytes 1474560
  1212.9 605.5 %reduce-scatter.61.cloned.1.call-start = ((), (), s32[]{:S(2)}) async-start(), calls=%async_computation.34 | async-start | bytes 1474560
  1346.3 552.0 %all-reduce.12.cloned.1.call-start = ((), (), s32[]{:S(2)}) async-start(), calls=%async_computation.47 | async-start | bytes 4718592
  1356.0 572.8 %reduce-scatter.51.cloned.1.call-start = ((), (), s32[]{:S(2)}) async-start(), calls=%async_computation.29 | async-start | bytes 1474560 | tf_op jit(solution)/shard_map/reduce_scatter | solution.py:368
  1356.6 602.5 %reduce-scatter.55.cloned.1.call-start = ((), (), s32[]{:S(2)}) async-start(), calls=%async_computation.31 | async-start | bytes 1474560 | tf_op jit(solution)/shard_map/reduce_scatter | solution.py:368
  (237 other events, 5102.7 us)
Sparse Core Ops, SparseCore 0:
  9.6 45.7 all-gather.9
  57.5 29.6 all-gather.13
  89.7 29.4 all-gather.7
  121.0 48.4 all-gather.17
  171.2 83.0 all-gather.11
  265.0 57.7 all-gather.15
  744.7 40.5 reduce-scatter.44
  802.2 40.9 reduce-scatter.46
  891.8 187.7 all-reduce.9
  1083.0 76.7 reduce-scatter.56
  1163.3 76.6 reduce-scatter.58
  1243.4 76.6 reduce-scatter.48
  1323.6 76.6 reduce-scatter.52
  1403.7 33.6 reduce-scatter.68
  1440.9 33.6 reduce-scatter.70
  1477.5 34.9 reduce-scatter.76
  1515.5 34.9 reduce-scatter.78
  1553.3 33.6 reduce-scatter.72
  1590.0 33.6 reduce-scatter.74
  1626.5 33.6 reduce-scatter.82
  1663.2 33.6 reduce-scatter.80
  1804.9 93.2 all-reduce.11
  1900.4 28.3 reduce-scatter.50
  1931.1 27.9 reduce-scatter.54
  (4 shorter events, 95.2 us)
